TPU v7x, 32 devices: a whole 2x2x4 slice. The times are simulated.
32 devices in a mesh: dp: 8 (over y, x, core), mp: 4 (over z).
Axes of the slice: x: 2, y: 2, z: 4, core: 2. Of those that a mesh axis runs over, the one named last changes fastest.
Arguments:
- x_in: bfloat16 [8192, 768], P(('dp', 'mp')), may hold values from -6 to 6
- enc_in: bfloat16 [4096, 768], P(('dp', 'mp')), may hold values from -6 to 6
- cotangent: bfloat16 [8192, 768], P(('dp', 'mp')), may hold values from -6 to 6
- dec_len: int32 [8], P('dp'), may hold values from 128 to 1024, as said below
- enc_len: int32 [8], P('dp'), may hold values from 64 to 512, as said below
- self_qkv: bfloat16 [768, 3, 768], P(None, None, 'mp'), may hold values from -0.109375 to 0.109375
- self_out: bfloat16 [768, 768], P('mp'), may hold values from -1.75 to 1.75
- cross_q: bfloat16 [768, 768], P(None, 'mp'), may hold values from -0.0546875 to 0.0546875
- cross_kv: bfloat16 [768, 2, 768], P(None, None, 'mp'), may hold values from -0.21875 to 0.21875
- cross_out: bfloat16 [768, 768], P('mp'), may hold values from -1.25 to 1.25
- ff_in: bfloat16 [768, 2, 2048], P(None, None, 'mp'), may hold values from -0.21875 to 0.21875
- ff_out: bfloat16 [2048, 768], P('mp'), may hold values from -0.1875 to 0.1875
- gains: bfloat16 [3, 768], replicated, may hold values from 0.5 to 1.5
- table: bfloat16 [32, 12], P(None, 'mp'), may hold values from -6 to 6
Outputs:
- layer_out: bfloat16 [8192, 768], P(('dp', 'mp'))
- input_grad: float32 [8192, 768], P(('dp', 'mp'))
- enc_grad: float32 [4096, 768], P(('dp', 'mp'))
- self_qkv_grad: float32 [768, 3, 768], P(None, None, 'mp')
- self_out_grad: float32 [768, 768], P('mp')
- cross_q_grad: float32 [768, 768], P(None, 'mp')
- cross_kv_grad: float32 [768, 2, 768], P(None, None, 'mp')
- cross_out_grad: float32 [768, 768], P('mp')
- ff_in_grad: float32 [768, 2, 2048], P(None, None, 'mp')
- ff_out_grad: float32 [2048, 768], P('mp')
- gains_grad: float32 [3, 768], replicated
- table_grad: float32 [32, 12], P(None, 'mp')
Inputs may be any that keep to these rules, and one draw needn't show every extreme that they name: dec_len[s] is the number of live decoder positions of sequence s; the sequences on one index of dp are of similar length; some sequence has exactly 1024. enc_len[s] is the number of live encoder positions of sequence s; some sequence has exactly 512.
All inputs are finite; a program needn't handle non-finite values.
Results may differ from a plain program's by a relative error of at most 0.035.
Values may be sent and summed in bfloat16 or wider, within the bound.
A program may use at most 192 MiB of HBM per device.

v0:
```python
import math
import jax
import jax.numpy as jnp
from jax import lax
from jax.sharding import PartitionSpec as P

NB = 32
MAXD = 128
LDEC = 1024
LENC = 512
NORM_EPS = 1e-06
MASK_FILL = -1000000000.0


def bucket_index(distance):
    half_count = NB // 2
    clipped = jnp.maximum(distance, 0)
    bucket_ids = jnp.minimum(clipped, half_count)
    for level_pos in range(1, half_count):
        threshold = math.ceil(half_count * (MAXD / half_count) ** (level_pos / half_count))
        bucket_ids = bucket_ids + (clipped >= threshold).astype(jnp.int32)
    return bucket_ids


def bucket_tiles(row_start, row_count, key_start, key_count, dtype):
    query_pos = row_start + lax.broadcasted_iota(jnp.int32, (row_count, key_count), 0)
    key_pos = key_start + lax.broadcasted_iota(jnp.int32, (row_count, key_count), 1)
    bucket_ids = bucket_index(query_pos - key_pos)
    levels = lax.broadcasted_iota(jnp.int32, (NB, row_count, key_count), 0)
    return (levels == bucket_ids[None]).astype(dtype)


def norm_forward(values, gain_row):
    inv_rms = lax.rsqrt(jnp.mean(values * values, axis=-1, keepdims=True) + NORM_EPS)
    return ((values * inv_rms * gain_row).astype(jnp.bfloat16), inv_rms)


def norm_backward(values, inv_rms, gain_row, upstream):
    scaled = upstream * gain_row
    grad_in = inv_rms * scaled - values * inv_rms**3 * jnp.mean(
        scaled * values, axis=-1, keepdims=True
    )
    grad_gain = jnp.sum(upstream * values * inv_rms, axis=0)
    return (grad_in, grad_gain)


def dot_first(left, right):
    return lax.dot_general(
        left, right, (((0,), (0,)), ((), ())), preferred_element_type=jnp.float32
    )


def dot_last(left, right):
    return lax.dot_general(
        left, right, (((1,), (1,)), ((), ())), preferred_element_type=jnp.float32
    )


def gelu_tanh(values):
    return jax.nn.gelu(values, approximate=True)


def gather_rows(normed):
    return lax.all_gather(normed, "mp", axis=0, tiled=True)


def gather_back(grad_rows):
    return lax.all_gather(grad_rows, "mp", axis=0, tiled=True)


def spread_rows(source, weight, rows_here):

    def product(row_start, row_count):
        return jnp.dot(source, weight, preferred_element_type=jnp.float32)

    return lax.psum_scatter(
        product(jnp.int32(0), rows_here * lax.axis_size("mp")),
        "mp",
        scatter_dimension=0,
        tiled=True,
    )


def spread_back(source, weight, rows_here):

    def product(row_start, row_count):
        return dot_last(source, weight)

    return lax.psum_scatter(
        product(jnp.int32(0), rows_here * lax.axis_size("mp")),
        "mp",
        scatter_dimension=0,
        tiled=True,
    )


def block_scores(block_q, key_rows, bias_block, allowed):
    scores = (
        jnp.einsum("qhd,khd->hqk", block_q, key_rows, preferred_element_type=jnp.float32)
        + bias_block
    )
    return jnp.where(allowed[None], scores, MASK_FILL)


def attention_forward(queries, key_rows, value_rows, bias_list, valid_fn):
    length = queries.shape[1]
    qblock = min(512, length)
    outputs = []
    totals = []
    for block_pos in range(length // qblock):
        row_start = block_pos * qblock
        block_q = queries[0, row_start : row_start + qblock]
        scores = block_scores(
            block_q, key_rows[0], bias_list[block_pos], valid_fn(0, row_start, qblock)
        )
        row_maximum_score = jnp.max(scores, axis=-1, keepdims=True)
        logsum = row_maximum_score + jnp.log(
            jnp.sum(jnp.exp(scores - row_maximum_score), axis=-1, keepdims=True)
        )
        weights_low = jnp.exp(scores - logsum).astype(jnp.bfloat16)
        attended = jnp.einsum(
            "hqk,khd->qhd", weights_low, value_rows[0], preferred_element_type=jnp.float32
        )
        outputs.append(attended.astype(jnp.bfloat16))
        totals.append(logsum)
    return (jnp.concatenate(outputs, axis=0), totals)


def attention_backward(
    queries, key_rows, value_rows, bias_list, valid_fn, totals, grad_out, keep_scores
):
    length = queries.shape[1]
    qblock = min(512, length)
    block_count = length // qblock
    grad_queries = []
    score_sums = [None] * block_count
    key_acc = jnp.zeros(key_rows.shape[1:], jnp.float32)
    value_running_total = jnp.zeros(value_rows.shape[1:], jnp.float32)
    for block_pos in range(block_count):
        row_start = block_pos * qblock
        block_q = queries[0, row_start : row_start + qblock]
        block_grad = grad_out[0, row_start : row_start + qblock]
        scores = block_scores(
            block_q, key_rows[0], bias_list[block_pos], valid_fn(0, row_start, qblock)
        )
        weights_full = jnp.exp(scores - totals[block_pos])
        weights_low = weights_full.astype(jnp.bfloat16)
        grad_weights = jnp.einsum(
            "qhd,khd->hqk", block_grad, value_rows[0], preferred_element_type=jnp.float32
        )
        row_inner = jnp.sum(weights_full * grad_weights, axis=-1, keepdims=True)
        grad_scores = (weights_full * (grad_weights - row_inner)).astype(jnp.bfloat16)
        grad_queries.append(
            jnp.einsum(
                "hqk,khd->qhd", grad_scores, key_rows[0], preferred_element_type=jnp.float32
            ).astype(jnp.bfloat16)
        )
        key_acc = key_acc + jnp.einsum(
            "hqk,qhd->khd", grad_scores, block_q, preferred_element_type=jnp.float32
        )
        value_running_total = value_running_total + jnp.einsum(
            "hqk,qhd->khd", weights_low, block_grad, preferred_element_type=jnp.float32
        )
        if keep_scores:
            score_part = grad_scores.astype(jnp.float32)
            score_sums[block_pos] = score_part
    grad_keys = key_acc.astype(jnp.bfloat16)
    grad_values = value_running_total.astype(jnp.bfloat16)
    return (jnp.concatenate(grad_queries, axis=0), grad_keys, grad_values, score_sums)


def local(
    x_in,
    enc_in,
    cotangent,
    dec_len,
    enc_len,
    self_qkv,
    self_out,
    cross_q,
    cross_kv,
    cross_out,
    ff_in,
    ff_out,
    gains,
    table,
):
    rows_here = x_in.shape[0]
    model_width = x_in.shape[1]
    seq_count = dec_len.shape[0]
    head_count = table.shape[1]
    head_cols = self_qkv.shape[2]
    head_size = head_cols // head_count
    hidden_cols = ff_in.shape[2]
    qblock = min(512, LDEC)
    key_block_span = min(256, LDEC)
    gain_rows = gains.astype(jnp.float32)
    resid_zero = x_in.astype(jnp.float32)
    qkv_matrix = self_qkv.reshape(model_width, 3 * head_cols)
    kv_matrix = cross_kv.reshape(model_width, 2 * head_cols)
    hidden_matrix = ff_in.reshape(model_width, 2 * hidden_cols)
    bias_blocks = []
    for block_pos in range(LDEC // qblock):
        pieces = []
        for key_pos in range(LDEC // key_block_span):
            indicator_matrix = bucket_tiles(
                block_pos * qblock, qblock, key_pos * key_block_span, key_block_span, jnp.bfloat16
            )
            pieces.append(
                jnp.einsum(
                    "dvj,dp->pvj", indicator_matrix, table, preferred_element_type=jnp.float32
                )
            )
        bias_blocks.append(jnp.concatenate(pieces, axis=2))
    zero_bias = [0.0] * (LDEC // qblock)

    def causal_valid(seq_pos, row_start, row_count):
        query_pos = row_start + lax.broadcasted_iota(jnp.int32, (row_count, LDEC), 0)
        key_pos = lax.broadcasted_iota(jnp.int32, (row_count, LDEC), 1)
        return (key_pos <= query_pos) & (key_pos < dec_len[seq_pos])

    def encoder_valid(seq_pos, row_start, row_count):
        key_pos = lax.broadcasted_iota(jnp.int32, (row_count, LENC), 1)
        return key_pos < enc_len[seq_pos]

    normed_one, inv_one = norm_forward(resid_zero, gain_rows[0])
    full_one = gather_rows(normed_one)
    qkv_one = jnp.dot(full_one, qkv_matrix, preferred_element_type=jnp.float32).astype(jnp.bfloat16)
    qkv_split = qkv_one.reshape(seq_count, LDEC, 3, head_count, head_size)
    query_one = qkv_split[:, :, 0]
    key_one = qkv_split[:, :, 1]
    value_one = qkv_split[:, :, 2]
    attended_one, totals_one = attention_forward(
        query_one, key_one, value_one, bias_blocks, causal_valid
    )
    attended_one = attended_one.reshape(seq_count * LDEC, head_cols)
    resid_one = resid_zero + spread_rows(attended_one, self_out, rows_here)
    normed_two, inv_two = norm_forward(resid_one, gain_rows[1])
    complete_second = gather_rows(normed_two)
    query_two = (
        jnp.dot(complete_second, cross_q, preferred_element_type=jnp.float32)
        .astype(jnp.bfloat16)
        .reshape(seq_count, LDEC, head_count, head_size)
    )
    enc_full = lax.all_gather(enc_in, "mp", axis=0, tiled=True)
    kv_two = (
        jnp.dot(enc_full, kv_matrix, preferred_element_type=jnp.float32)
        .astype(jnp.bfloat16)
        .reshape(seq_count, LENC, 2, head_count, head_size)
    )
    key_two = kv_two[:, :, 0]
    value_two = kv_two[:, :, 1]
    attended_two, totals_two = attention_forward(
        query_two, key_two, value_two, zero_bias, encoder_valid
    )
    attended_two = attended_two.reshape(seq_count * LDEC, head_cols)
    resid_two = resid_one + spread_rows(attended_two, cross_out, rows_here)
    normed_three, inv_three = norm_forward(resid_two, gain_rows[2])
    full_three = gather_rows(normed_three)
    gate_up = jnp.dot(full_three, hidden_matrix, preferred_element_type=jnp.float32)
    gate_part = gate_up[:, :hidden_cols]
    up_part = gate_up[:, hidden_cols:]
    gelu_value, gelu_cotangent_map = jax.vjp(gelu_tanh, gate_part)
    activated = (gelu_value * up_part).astype(jnp.bfloat16)
    layer_out = resid_two + spread_rows(activated, ff_out, rows_here)
    grad_three = cotangent.astype(jnp.float32)
    back_three = gather_back(grad_three.astype(jnp.bfloat16))
    ff_out_grad = dot_first(activated, back_three)
    grad_act = dot_last(back_three, ff_out)
    grad_gate = gelu_cotangent_map(grad_act * up_part)[0]
    grad_hidden = jnp.concatenate([grad_gate, grad_act * gelu_value], axis=1).astype(jnp.bfloat16)
    ff_in_grad = dot_first(full_three, grad_hidden).reshape(model_width, 2, hidden_cols)
    norm_part, gain_three = norm_backward(
        resid_two, inv_three, gain_rows[2], spread_back(grad_hidden, hidden_matrix, rows_here)
    )
    grad_two = grad_three + norm_part
    back_two = gather_back(grad_two.astype(jnp.bfloat16))
    cross_out_grad = dot_first(attended_two, back_two)
    grad_att_two = (
        dot_last(back_two, cross_out)
        .astype(jnp.bfloat16)
        .reshape(seq_count, LDEC, head_count, head_size)
    )
    grad_query_two, grad_key_two, grad_value_two, unused = attention_backward(
        query_two, key_two, value_two, zero_bias, encoder_valid, totals_two, grad_att_two, False
    )
    grad_query_two = grad_query_two.reshape(seq_count * LDEC, head_cols)
    grad_kv = jnp.stack([grad_key_two, grad_value_two], axis=1).reshape(
        seq_count * LENC, 2 * head_cols
    )
    cross_q_grad = dot_first(complete_second, grad_query_two)
    cross_kv_grad = dot_first(enc_full, grad_kv).reshape(model_width, 2, head_cols)
    enc_grad = lax.psum_scatter(dot_last(grad_kv, kv_matrix), "mp", scatter_dimension=0, tiled=True)
    norm_part, gain_two = norm_backward(
        resid_one, inv_two, gain_rows[1], spread_back(grad_query_two, cross_q, rows_here)
    )
    grad_one = grad_two + norm_part
    back_one = gather_back(grad_one.astype(jnp.bfloat16))
    self_out_grad = dot_first(attended_one, back_one)
    grad_att_one = (
        dot_last(back_one, self_out)
        .astype(jnp.bfloat16)
        .reshape(seq_count, LDEC, head_count, head_size)
    )
    grad_query_one, grad_key_one, grad_value_one, score_sums = attention_backward(
        query_one, key_one, value_one, bias_blocks, causal_valid, totals_one, grad_att_one, True
    )
    grad_qkv = jnp.stack([grad_query_one, grad_key_one, grad_value_one], axis=1).reshape(
        seq_count * LDEC, 3 * head_cols
    )
    self_qkv_grad = dot_first(full_one, grad_qkv).reshape(model_width, 3, head_cols)
    table_grad = jnp.zeros((table.shape[0], head_count), jnp.float32)
    for block_pos in range(LDEC // qblock):
        for key_pos in range(LDEC // key_block_span):
            indicator_matrix = bucket_tiles(
                block_pos * qblock, qblock, key_pos * key_block_span, key_block_span, jnp.float32
            )
            score_tile = score_sums[block_pos][
                :, :, key_pos * key_block_span : (key_pos + 1) * key_block_span
            ]
            table_grad = table_grad + jnp.einsum(
                "gfy,pfy->pg",
                score_tile,
                indicator_matrix,
                precision=lax.Precision.HIGHEST,
                preferred_element_type=jnp.float32,
            )
    norm_part, gain_one = norm_backward(
        resid_zero, inv_one, gain_rows[0], spread_back(grad_qkv, qkv_matrix, rows_here)
    )
    input_grad = grad_one + norm_part
    (
        self_qkv_grad,
        self_out_grad,
        cross_q_grad,
        cross_kv_grad,
        cross_out_grad,
        ff_in_grad,
        ff_out_grad,
        table_grad,
    ) = lax.psum(
        (
            self_qkv_grad,
            self_out_grad,
            cross_q_grad,
            cross_kv_grad,
            cross_out_grad,
            ff_in_grad,
            ff_out_grad,
            table_grad,
        ),
        "dp",
    )
    gains_grad = lax.psum(jnp.stack([gain_one, gain_two, gain_three]), ("dp", "mp"))
    return (
        layer_out.astype(jnp.bfloat16),
        input_grad,
        enc_grad,
        self_qkv_grad,
        self_out_grad,
        cross_q_grad,
        cross_kv_grad,
        cross_out_grad,
        ff_in_grad,
        ff_out_grad,
        gains_grad,
        table_grad,
    )


def solution(mesh):
    in_specs = (
        P(("dp", "mp"), None),
        P(("dp", "mp"), None),
        P(("dp", "mp"), None),
        P("dp"),
        P("dp"),
        P(None, None, "mp"),
        P("mp", None),
        P(None, "mp"),
        P(None, None, "mp"),
        P("mp", None),
        P(None, None, "mp"),
        P("mp", None),
        P(),
        P(None, "mp"),
    )
    out_specs = (
        P(("dp", "mp"), None),
        P(("dp", "mp"), None),
        P(("dp", "mp"), None),
        P(None, None, "mp"),
        P("mp", None),
        P(None, "mp"),
        P(None, None, "mp"),
        P("mp", None),
        P(None, None, "mp"),
        P("mp", None),
        P(),
        P(None, "mp"),
    )
    return jax.shard_map(local, mesh=mesh, in_specs=in_specs, out_specs=out_specs, check_vma=False)
```

profile of v0, /device:TPU:0, one launch (start us, length us, event | category | flops | bytes accessed | tf_op | source)
XLA Modules:
  0.0 903.8 jit_solution(2324097600538504131)
XLA Ops:
  13.9 3.2 fusion.15
  17.5 6.0 convert_add_fusion.1
  71.8 62.7 %reduce-scatter.8.cloned.1.call-done = f32[256,768]{1,0:T(8,128)} async-done(((f32[1024,768]{1,0:T(8,128)}), f32[256,768]{1,0:T(8,128)}) %reduce-scatter.8.cloned.1.call-update) | async-done | bytes 786448 | tf_op jit(solution)/shard_map/reduce_scatter | solution.py:76
  138.0 24.3 %all_gather.22 = bf16[512,768]{1,0:T(8,128)(2,1)S(1)} all-gather(bf16[128,768]{1,0:T(8,128)(2,1)S(1)} %copy-done.76), channel_id=1, replica_groups=mesh['dp'=8,'mp'=4] {'mp'}, dimensions={0}, use_global_device_ids=true | all-gather | bytes 983040 | tf_op jit(solution)/shard_map/all_gather | solution.py:245
  162.9 17.9 %all-gather.9.cloned.1.call-done = bf16[1024,768]{1,0:T(8,128)(2,1)} async-done(((bf16[256,768]{1,0:T(8,128)(2,1)}), bf16[1024,768]{1,0:T(8,128)(2,1)}) %all-gather.9.cloned.1.call-update) | async-done | bytes 1572880 | tf_op jit(solution)/shard_map/all_gather | solution.py:64
  191.9 60.2 %reduce-scatter.10.cloned.1.call-done = f32[256,768]{1,0:T(8,128)} async-done(((f32[1024,768]{1,0:T(8,128)}), f32[256,768]{1,0:T(8,128)}) %reduce-scatter.10.cloned.1.call-update) | async-done | bytes 786448 | tf_op jit(solution)/shard_map/reduce_scatter | solution.py:76
  255.7 3.0 copy.58
  258.7 33.5 %all-gather.11.cloned.1.call-done = bf16[1024,768]{1,0:T(8,128)(2,1)} async-done(((bf16[256,768]{1,0:T(8,128)(2,1)}), bf16[1024,768]{1,0:T(8,128)(2,1)}) %all-gather.11.cloned.1.call-update) | async-done | bytes 1572880 | tf_op jit(solution)/shard_map/all_gather | solution.py:64
  292.2 5.8 fusion.305
  298.0 31.6 %all-gather.13.cloned.1.call-done = bf16[1024,768]{1,0:T(8,128)(2,1)} async-done(((bf16[256,768]{1,0:T(8,128)(2,1)}), bf16[1024,768]{1,0:T(8,128)(2,1)}) %all-gather.13.cloned.1.call-update) | async-done | bytes 1572880 | tf_op jit(solution)/shard_map/all_gather | solution.py:68
  329.6 6.4 fusion.42
  337.3 3.5 fusion.50
  340.9 4.1 fusion.306
  345.0 55.1 %reduce-scatter.14.cloned.1.call-done = f32[256,768]{1,0:T(8,128)} async-done(((f32[1024,768]{1,0:T(8,128)}), f32[256,768]{1,0:T(8,128)}) %reduce-scatter.14.cloned.1.call-update) | async-done | bytes 786448 | tf_op jit(solution)/shard_map/reduce_scatter | solution.py:89
  402.6 60.1 %reduce-scatter.12.cloned.1.call-done = f32[256,768]{1,0:T(8,128)} async-done(((f32[1024,768]{1,0:T(8,128)}), f32[256,768]{1,0:T(8,128)}) %reduce-scatter.12.cloned.1.call-update) | async-done | bytes 786448 | tf_op jit(solution)/shard_map/reduce_scatter | solution.py:76
  465.6 37.2 %all-gather.15.cloned.1.call-done = bf16[1024,768]{1,0:T(8,128)(2,1)} async-done(((bf16[256,768]{1,0:T(8,128)(2,1)}), bf16[1024,768]{1,0:T(8,128)(2,1)}) %all-gather.15.cloned.1.call-update) | async-done | bytes 1572880 | tf_op jit(solution)/shard_map/all_gather | solution.py:68
  505.8 3.5 multiply_reduce_fusion.3
  516.9 58.8 %reduce-scatter.16.cloned.1.call-done = f32[256,768]{1,0:T(8,128)} async-done(((f32[1024,768]{1,0:T(8,128)}), f32[256,768]{1,0:T(8,128)}) %reduce-scatter.16.cloned.1.call-update) | async-done | bytes 786448 | tf_op jit(solution)/shard_map/reduce_scatter | solution.py:89
  580.3 37.2 %all-gather.17.cloned.1.call-done = bf16[1024,768]{1,0:T(8,128)(2,1)} async-done(((bf16[256,768]{1,0:T(8,128)(2,1)}), bf16[1024,768]{1,0:T(8,128)(2,1)}) %all-gather.17.cloned.1.call-update) | async-done | bytes 1572880 | tf_op jit(solution)/shard_map/all_gather | solution.py:68
  619.7 4.1 fusion.92
  623.8 3.9 multiply_reduce_fusion
  639.9 3.1 fusion.308
  650.9 5.1 fusion.49
  656.1 5.8 reshape.765
  661.9 3.7 fusion.313
  683.8 3.1 fusion.80
  692.7 2.9 fusion.77
  695.6 3.1 fusion.76
  701.6 14.0 %psum.71 = f32[32,3]{0,1:T(4,128)} all-reduce(f32[32,3]{0,1:T(4,128)S(1)} %fusion.75), channel_id=1, replica_groups=mesh['dp'=8,'mp'=4] {'dp'}, use_global_device_ids=true, to_apply=%region_36.37 | all-reduce | flops 96 | bytes 768 | tf_op jit(solution)/shard_map/psum | solution.py:341
  717.1 39.5 %psum.70 = f32[3,768]{1,0:T(4,128)} all-reduce(f32[3,768]{1,0:T(4,128)S(1)} %pad_maximum_fusion.8), channel_id=1, replica_groups=mesh['dp'=8,'mp'=4] {'dp','mp'}, use_global_device_ids=true, to_apply=%region_35.36 | all-reduce | flops 2304 | bytes 18432 | tf_op jit(solution)/shard_map/psum | solution.py:354
  758.9 127.8 %all-reduce.3.cloned.1.call-done = (f32[768,3,192]{0,2,1:T(8,128)}, f32[192,768]{1,0:T(8,128)}, f32[768,192]{0,1:T(8,128)}, f32[768,2,192]{0,2,1:T(8,128)}, f32[...) async-done(((f32[768,3,192]{0,2,1:T(8,128)}, f32[192,768]{1,0:T(8,128)}, f32[768,192]{0,1:T(8,128)}, f32[768,2,192]{0,2,1:T(8,128)}, ...) | async-done | bytes 9437200 | tf_op jit(solution)/shard_map/psum | solution.py:341
  886.7 2.9 copy.100
  (364 shorter events, 153.6 us)
Async XLA Ops:
  7.2 45.6 %copy-start = (bf16[768,3,192]{0,2,1:T(8,128)(2,1)S(1)}, bf16[768,3,192]{0,2,1:T(8,128)(2,1)}, u32[]{:S(2)}) copy-start(bf16[768,3,192]{0,2,1:T(8,128)(2,1)} %param.19) | copy-start | bytes 2654212
  7.2 45.6 %all-gather.7.cloned.1.call-start = ((), (), s32[]{:S(2)}) async-start(), calls=%async_computation.7 | async-start | bytes 1966080 | tf_op jit(solution)/shard_map/all_gather | solution.py:64
  10.4 126.0 %copy-start.88 = (f32[768]{0:T(1024)}, f32[768]{0:T(1024)S(1)}, u32[]{:S(2)}) copy-start(f32[768]{0:T(1024)S(1)} %get-tuple-element.19) | copy-start | bytes 9220
  12.9 121.6 %reduce-scatter.8.cloned.1.call-start = ((), (), s32[]{:S(2)}) async-start(), calls=%async_computation.8 | async-start | bytes 3932160 | tf_op jit(solution)/shard_map/reduce_scatter | solution.py:76
  23.5 24.4 %copy-start.68 = (s32[512,256]{1,0:T(8,128)}, s32[512,256]{1,0:T(8,128)S(1)}, u32[]{:S(2)}) copy-start(s32[512,256]{1,0:T(8,128)S(1)} %get-tuple-element.58) | copy-start | bytes 1572868
  69.4 65.1 %copy-start.13 = (bf16[256,768]{1,0:T(8,128)(2,1)S(1)}, bf16[256,768]{1,0:T(8,128)(2,1)}, u32[]{:S(2)}) copy-start(bf16[256,768]{1,0:T(8,128)(2,1)} %param.14) | copy-start | bytes 1179652
  71.7 66.3 %copy-start.76 = (bf16[128,768]{1,0:T(8,128)(2,1)S(1)}, bf16[128,768]{1,0:T(8,128)(2,1)}, u32[]{:S(2)}) copy-start(bf16[128,768]{1,0:T(8,128)(2,1)} %param.15) | copy-start | bytes 589828
  71.7 90.7 %copy-start.51 = (bf16[768,2,192]{0,2,1:T(8,128)(2,1)S(1)}, bf16[768,2,192]{0,2,1:T(8,128)(2,1)}, u32[]{:S(2)}) copy-start(bf16[768,2,192]{0,2,1:T(8,128)(2,1)} %param.22) | copy-start | bytes 1769476
  71.7 109.0 %all-gather.9.cloned.1.call-start = ((), (), s32[]{:S(2)}) async-start(), calls=%async_computation.9 | async-start | bytes 1966080 | tf_op jit(solution)/shard_map/all_gather | solution.py:64
  136.4 46.5 %copy-start.98 = (f32[256]{0:T(256)}, f32[256]{0:T(256)S(1)}, u32[]{:S(2)}) copy-start(f32[256]{0:T(256)S(1)} %get-tuple-element.62) | copy-start | bytes 3076
  137.3 114.8 %reduce-scatter.10.cloned.1.call-start = ((), (), s32[]{:S(2)}) async-start(), calls=%async_computation.10 | async-start | bytes 3932160 | tf_op jit(solution)/shard_map/reduce_scatter | solution.py:76
  138.0 46.9 %copy-start.89 = (pred[512]{0:T(512)(128)(4,1)}, pred[512]{0:T(512)(128)(4,1)S(1)}, u32[]{:S(2)}) copy-start(pred[512]{0:T(512)(128)(4,1)S(1)} %iota_compare_fusion.57) | copy-start | bytes 1540
  162.9 342.8 %copy-start.23 = (bf16[512,384]{0,1:T(8,128)(2,1)}, bf16[512,384]{0,1:T(8,128)(2,1)S(1)}, u32[]{:S(2)}) copy-start(bf16[512,384]{0,1:T(8,128)(2,1)S(1)} %convolution_convert_fusion.4) | copy-start | bytes 1179652
  191.8 62.2 %copy-start.87 = (f32[768]{0:T(1024)S(1)}, f32[768]{0:T(1024)}, u32[]{:S(2)}) copy-start(f32[768]{0:T(1024)} %get-tuple-element.18) | copy-start | bytes 9220
  191.9 100.3 %all-gather.11.cloned.1.call-start = ((), (), s32[]{:S(2)}) async-start(), calls=%async_computation.11 | async-start | bytes 1966080 | tf_op jit(solution)/shard_map/all_gather | solution.py:64
  254.0 44.0 %copy-start.99 = (f32[256]{0:T(256)}, f32[256]{0:T(256)S(1)}, u32[]{:S(2)}) copy-start(f32[256]{0:T(256)S(1)} %get-tuple-element.64) | copy-start | bytes 3076
  254.9 74.7 %all-gather.13.cloned.1.call-start = ((), (), s32[]{:S(2)}) async-start(), calls=%async_computation.13 | async-start | bytes 1966080 | tf_op jit(solution)/shard_map/all_gather | solution.py:68
  255.5 144.6 %reduce-scatter.14.cloned.1.call-start = ((), (), s32[]{:S(2)}) async-start(), calls=%async_computation.14 | async-start | bytes 3932160 | tf_op jit(solution)/shard_map/reduce_scatter | solution.py:89
  340.8 121.9 %reduce-scatter.12.cloned.1.call-start = ((), (), s32[]{:S(2)}) async-start(), calls=%async_computation.12 | async-start | bytes 3932160 | tf_op jit(solution)/shard_map/reduce_scatter | solution.py:76
  345.0 117.8 %copy-start.46 = (bf16[256,768]{1,0:T(8,128)(2,1)S(1)}, bf16[256,768]{1,0:T(8,128)(2,1)}, u32[]{:S(2)}) copy-start(bf16[256,768]{1,0:T(8,128)(2,1)} %param.16) | copy-start | bytes 1179652
  345.0 157.9 %all-gather.15.cloned.1.call-start = ((), (), s32[]{:S(2)}) async-start(), calls=%async_computation.15 | async-start | bytes 1966080 | tf_op jit(solution)/shard_map/all_gather | solution.py:68
  465.6 40.2 %copy-start.78 = (f32[3,512]{1,0:T(4,128)S(1)}, f32[3,512]{1,0:T(4,128)}, u32[]{:S(2)}) copy-start(f32[3,512]{1,0:T(4,128)} %copy-done.77) | copy-start | bytes 18436
  465.6 40.2 %copy-start.82 = (f32[3,512]{1,0:T(4,128)S(1)}, f32[3,512]{1,0:T(4,128)}, u32[]{:S(2)}) copy-start(f32[3,512]{1,0:T(4,128)} %copy-done.81) | copy-start | bytes 18436
  465.6 40.2 %copy-start.91 = (pred[512]{0:T(512)(128)(4,1)S(1)}, pred[512]{0:T(512)(128)(4,1)}, u32[]{:S(2)}) copy-start(pred[512]{0:T(512)(128)(4,1)} %copy-done.89) | copy-start | bytes 1540
  465.6 110.1 %reduce-scatter.16.cloned.1.call-start = ((), (), s32[]{:S(2)}) async-start(), calls=%async_computation.16 | async-start | bytes 3932160 | tf_op jit(solution)/shard_map/reduce_scatter | solution.py:89
  516.4 101.2 %copy-start.75 = (bf16[192,768]{1,0:T(8,128)(2,1)S(1)}, bf16[192,768]{1,0:T(8,128)(2,1)}, u32[]{:S(2)}) copy-start(bf16[192,768]{1,0:T(8,128)(2,1)} %param.20) | copy-start | bytes 884740
  516.4 101.1 %all-gather.17.cloned.1.call-start = ((), (), s32[]{:S(2)}) async-start(), calls=%async_computation.17 | async-start | bytes 1966080 | tf_op jit(solution)/shard_map/all_gather | solution.py:68
  580.3 135.4 %reduce-scatter.18.cloned.1.call-start = ((), (), s32[]{:S(2)}) async-start(), calls=%async_computation.18 | async-start | bytes 3932160 | tf_op jit(solution)/shard_map/reduce_scatter | solution.py:89
  643.0 115.8 %reduce-scatter.20.cloned.1.call-start = ((), (), s32[]{:S(2)}) async-start(), calls=%async_computation.19 | async-start | bytes 1966080 | tf_op jit(solution)/shard_map/reduce_scatter | solution.py:293
  650.9 235.8 %all-reduce.3.cloned.1.call-start = ((), (), s32[]{:S(2)}) async-start(), calls=%async_computation.20 | async-start | bytes 18874368 | tf_op jit(solution)/shard_map/psum | solution.py:341
  698.7 57.9 %copy-start.28 = (f32[256,768]{1,0:T(8,128)S(1)}, f32[256,768]{1,0:T(8,128)}, u32[]{:S(2)}) copy-start(f32[256,768]{1,0:T(8,128)} %get-tuple-element.33) | copy-start | bytes 2359300
  698.7 57.9 %copy-start.100 = (f32[256]{0:T(256)S(1)}, f32[256]{0:T(256)}, u32[]{:S(2)}) copy-start(f32[256]{0:T(256)} %get-tuple-element.59) | copy-start | bytes 3076
  (92 other events, 391.4 us)
Sparse Core Ops, SparseCore 0:
  13.0 39.7 all-gather.6
  71.8 62.5 reduce-scatter.7
  137.4 43.3 all-gather.8
  192.0 60.0 reduce-scatter.9
  255.0 37.1 all-gather.10
  293.6 35.9 all-gather.12
  341.0 59.1 reduce-scatter.13
  402.4 60.2 reduce-scatter.11
  465.7 37.0 all-gather.14
  516.5 59.1 reduce-scatter.15
  580.4 37.0 all-gather.16
  643.2 59.1 reduce-scatter.17
  705.8 35.8 reduce-scatter.19
  746.9 139.7 all-reduce.2
where the time goes:
time: 914 us; the launch traced here: 904 us
  waiting for transfers between devices  583 us (64%)
  matrix products  137 us (15%)
  blocking collectives  77.9 us (9%)
  local copies, waits for them, and re-layouts  48 us (5%)
  other arithmetic  39.2 us (4%)
  between operations  16.9 us (2%)
    reduce_scatter x3, waiting for transfers between devices, spread_rows(): lax.psum_scatter(product(jnp.int32(0), rows_here * lax.axis_size('mp')),...  183 us
    psum x1, waiting for transfers between devices, local(): lax.psum((self_qkv_grad, self_out_grad, cross_q_grad, cross_kv_grad, cros...  128 us
    reduce_scatter x3, waiting for transfers between devices, spread_back(): lax.psum_scatter(product(jnp.int32(0), rows_here * lax.axis_size('mp')),...  114 us
    all_gather x3, waiting for transfers between devices, gather_back(): return lax.all_gather(grad_rows, 'mp', axis=0, tiled=True)  106 us
    all_gather x3, waiting for transfers between devices, gather_rows(): return lax.all_gather(normed, 'mp', axis=0, tiled=True)  51.8 us
    psum x1, blocking collectives, local(): lax.psum(jnp.stack([gain_one, gain_two, gain_three]), ('dp', 'mp'))  39.5 us
    unnamed x228, local copies, waits for them, and re-layouts  28.4 us
    all_gather x1, blocking collectives, local(): enc_full = lax.all_gather(enc_in, 'mp', axis=0, tiled=True)  24.3 us
  transfers between devices with their start and end apart: 14, of which 12 were waited for; matrix products, arithmetic and copies ran while one was open for 13% of the time, Pallas kernels for 0%

commit v1 on v0

--- a/solution.py
+++ b/solution.py
@@ -242,7 +242,16 @@
         .astype(jnp.bfloat16)
         .reshape(seq_count, LDEC, head_count, head_size)
     )
-    enc_full = lax.all_gather(enc_in, "mp", axis=0, tiled=True)
+    ways = lax.axis_size("mp")
+    up = [(d, (d + 1) % ways) for d in range(ways)]
+    down = [(d, (d - 1) % ways) for d in range(ways)]
+    earlier, later = ([enc_in], [enc_in])
+    for _ in range(ways // 2):
+        earlier.append(lax.ppermute(earlier[-1], "mp", up))
+    for _ in range((ways - 1) // 2):
+        later.append(lax.ppermute(later[-1], "mp", down))
+    line = jnp.concatenate([*earlier[::-1], *later[1:]], axis=0)
+    enc_full = jnp.roll(line, (lax.axis_index("mp") - ways // 2) * enc_in.shape[0], axis=0)
     kv_two = (
         jnp.dot(enc_full, kv_matrix, preferred_element_type=jnp.float32)
         .astype(jnp.bfloat16)

time: 914 us -> 914 us (level)
  blocking collectives: 77.9 us -> 53.7 us
  waiting for transfers between devices: 583 us -> 602 us
    all_gather x1 -> x0, blocking collectives: 24.3 us -> none  [local(): enc_full = lax.all_gather(enc_in, 'mp', axis=0, tiled=True)]
    ppermute x0 -> x3, waiting for transfers between devices: none -> 21.4 us  [the longest x2 16.3 us: local(): earlier.append(lax.ppermute(earlier[-1], 'mp', up))]
    unnamed x228 -> x235, local copies, waits for them, and re-layouts: 28.4 us -> 29.7 us
  transfers between devices with their start and end apart: 14 -> 17, of which waited for: 12 -> 15; matrix products, arithmetic and copies ran while one was open for 13% -> 13% of each run, Pallas kernels for 0% -> 0%
where the time goes in v1:
time: 914 us; the launch traced here: 905 us
  waiting for transfers between devices  602 us (66%)
  matrix products  137 us (15%)
  blocking collectives  53.7 us (6%)
  local copies, waits for them, and re-layouts  49.5 us (5%)
  other arithmetic  39.2 us (4%)
  between operations  17 us (2%)
    reduce_scatter x3, waiting for transfers between devices, spread_rows(): lax.psum_scatter(product(jnp.int32(0), rows_here * lax.axis_size('mp')),...  183 us
    psum x1, waiting for transfers between devices, local(): lax.psum((self_qkv_grad, self_out_grad, cross_q_grad, cross_kv_grad, cros...  128 us
    reduce_scatter x3, waiting for transfers between devices, spread_back(): lax.psum_scatter(product(jnp.int32(0), rows_here * lax.axis_size('mp')),...  114 us
    all_gather x3, waiting for transfers between devices, gather_back(): return lax.all_gather(grad_rows, 'mp', axis=0, tiled=True)  106 us
    all_gather x3, waiting for transfers between devices, gather_rows(): return lax.all_gather(normed, 'mp', axis=0, tiled=True)  48.9 us
    psum x1, blocking collectives, local(): lax.psum(jnp.stack([gain_one, gain_two, gain_three]), ('dp', 'mp'))  39.7 us
    unnamed x235, local copies, waits for them, and re-layouts  29.7 us
    dot_general x8, matrix products, local(): jnp.einsum('gfy,pfy->pg', score_tile, indicator_matrix, precision=lax.Pre...  23.5 us
  transfers between devices with their start and end apart: 17, of which 15 were waited for; matrix products, arithmetic and copies ran while one was open for 13% of the time, Pallas kernels for 0%

profile of v1, /device:TPU:0, one launch (start us, length us, event | category | flops | bytes accessed | tf_op | source)
XLA Modules:
  0.0 904.7 jit_solution(5327022449811587826)
XLA Ops:
  13.9 3.2 fusion.15
  17.5 6.0 convert_add_fusion.1
  71.9 62.7 %reduce-scatter.8.cloned.1.call-done = f32[256,768]{1,0:T(8,128)} async-done(((f32[1024,768]{1,0:T(8,128)}), f32[256,768]{1,0:T(8,128)}) %reduce-scatter.8.cloned.1.call-update) | async-done | bytes 786448 | tf_op jit(solution)/shard_map/reduce_scatter | solution.py:76
  138.5 7.3 collective-permute-done
  145.8 3.8 collective-permute-start.2
  150.3 9.0 collective-permute-done.1
  159.3 5.1 collective-permute-done.2
  166.2 15.1 %all-gather.9.cloned.1.call-done = bf16[1024,768]{1,0:T(8,128)(2,1)} async-done(((bf16[256,768]{1,0:T(8,128)(2,1)}), bf16[1024,768]{1,0:T(8,128)(2,1)}) %all-gather.9.cloned.1.call-update) | async-done | bytes 1572880 | tf_op jit(solution)/shard_map/all_gather | solution.py:64
  192.4 60.6 %reduce-scatter.10.cloned.1.call-done = f32[256,768]{1,0:T(8,128)} async-done(((f32[1024,768]{1,0:T(8,128)}), f32[256,768]{1,0:T(8,128)}) %reduce-scatter.10.cloned.1.call-update) | async-done | bytes 786448 | tf_op jit(solution)/shard_map/reduce_scatter | solution.py:76
  259.5 33.5 %all-gather.11.cloned.1.call-done = bf16[1024,768]{1,0:T(8,128)(2,1)} async-done(((bf16[256,768]{1,0:T(8,128)(2,1)}), bf16[1024,768]{1,0:T(8,128)(2,1)}) %all-gather.11.cloned.1.call-update) | async-done | bytes 1572880 | tf_op jit(solution)/shard_map/all_gather | solution.py:64
  293.0 5.7 fusion.311
  298.7 31.7 %all-gather.13.cloned.1.call-done = bf16[1024,768]{1,0:T(8,128)(2,1)} async-done(((bf16[256,768]{1,0:T(8,128)(2,1)}), bf16[1024,768]{1,0:T(8,128)(2,1)}) %all-gather.13.cloned.1.call-update) | async-done | bytes 1572880 | tf_op jit(solution)/shard_map/all_gather | solution.py:68
  330.5 6.4 fusion.42
  338.1 3.5 fusion.50
  341.7 4.1 fusion.312
  345.9 55.1 %reduce-scatter.14.cloned.1.call-done = f32[256,768]{1,0:T(8,128)} async-done(((f32[1024,768]{1,0:T(8,128)}), f32[256,768]{1,0:T(8,128)}) %reduce-scatter.14.cloned.1.call-update) | async-done | bytes 786448 | tf_op jit(solution)/shard_map/reduce_scatter | solution.py:89
  403.5 60.1 %reduce-scatter.12.cloned.1.call-done = f32[256,768]{1,0:T(8,128)} async-done(((f32[1024,768]{1,0:T(8,128)}), f32[256,768]{1,0:T(8,128)}) %reduce-scatter.12.cloned.1.call-update) | async-done | bytes 786448 | tf_op jit(solution)/shard_map/reduce_scatter | solution.py:76
  466.5 37.2 %all-gather.15.cloned.1.call-done = bf16[1024,768]{1,0:T(8,128)(2,1)} async-done(((bf16[256,768]{1,0:T(8,128)(2,1)}), bf16[1024,768]{1,0:T(8,128)(2,1)}) %all-gather.15.cloned.1.call-update) | async-done | bytes 1572880 | tf_op jit(solution)/shard_map/all_gather | solution.py:68
  506.7 3.5 multiply_reduce_fusion.3
  517.7 58.8 %reduce-scatter.16.cloned.1.call-done = f32[256,768]{1,0:T(8,128)} async-done(((f32[1024,768]{1,0:T(8,128)}), f32[256,768]{1,0:T(8,128)}) %reduce-scatter.16.cloned.1.call-update) | async-done | bytes 786448 | tf_op jit(solution)/shard_map/reduce_scatter | solution.py:89
  581.2 37.2 %all-gather.17.cloned.1.call-done = bf16[1024,768]{1,0:T(8,128)(2,1)} async-done(((bf16[256,768]{1,0:T(8,128)(2,1)}), bf16[1024,768]{1,0:T(8,128)(2,1)}) %all-gather.17.cloned.1.call-update) | async-done | bytes 1572880 | tf_op jit(solution)/shard_map/all_gather | solution.py:68
  620.5 4.1 fusion.92
  624.6 3.9 multiply_reduce_fusion
  640.8 3.1 fusion.314
  651.8 5.1 fusion.49
  656.9 5.9 reshape.763
  662.8 3.7 fusion.318
  684.6 3.1 fusion.80
  696.4 3.1 fusion.76
  702.5 14.0 %psum.71 = f32[32,3]{0,1:T(4,128)} all-reduce(f32[32,3]{0,1:T(4,128)S(1)} %fusion.75), channel_id=1, replica_groups=mesh['dp'=8,'mp'=4] {'dp'}, use_global_device_ids=true, to_apply=%region_36.37 | all-reduce | flops 96 | bytes 768 | tf_op jit(solution)/shard_map/psum | solution.py:350
  717.9 39.7 %psum.70 = f32[3,768]{1,0:T(4,128)} all-reduce(f32[3,768]{1,0:T(4,128)S(1)} %pad_maximum_fusion.8), channel_id=1, replica_groups=mesh['dp'=8,'mp'=4] {'dp','mp'}, use_global_device_ids=true, to_apply=%region_35.36 | all-reduce | flops 2304 | bytes 18432 | tf_op jit(solution)/shard_map/psum | solution.py:363
  759.9 127.7 %all-reduce.3.cloned.1.call-done = (f32[768,3,192]{0,2,1:T(8,128)}, f32[192,768]{1,0:T(8,128)}, f32[768,192]{0,1:T(8,128)}, f32[768,2,192]{0,2,1:T(8,128)}, f32[...) async-done(((f32[768,3,192]{0,2,1:T(8,128)}, f32[192,768]{1,0:T(8,128)}, f32[768,192]{0,1:T(8,128)}, f32[768,2,192]{0,2,1:T(8,128)}, ...) | async-done | bytes 9437200 | tf_op jit(solution)/shard_map/psum | solution.py:350
  (377 shorter events, 164.8 us)
Async XLA Ops:
  7.2 45.7 %copy-start = (bf16[768,3,192]{0,2,1:T(8,128)(2,1)S(1)}, bf16[768,3,192]{0,2,1:T(8,128)(2,1)}, u32[]{:S(2)}) copy-start(bf16[768,3,192]{0,2,1:T(8,128)(2,1)} %param.19) | copy-start | bytes 2654212
  7.2 45.6 %all-gather.7.cloned.1.call-start = ((), (), s32[]{:S(2)}) async-start(), calls=%async_computation.7 | async-start | bytes 1966080 | tf_op jit(solution)/shard_map/all_gather | solution.py:64
  10.4 126.1 %copy-start.88 = (f32[768]{0:T(1024)}, f32[768]{0:T(1024)S(1)}, u32[]{:S(2)}) copy-start(f32[768]{0:T(1024)S(1)} %get-tuple-element.19) | copy-start | bytes 9220
  12.9 121.7 %reduce-scatter.8.cloned.1.call-start = ((), (), s32[]{:S(2)}) async-start(), calls=%async_computation.8 | async-start | bytes 3932160 | tf_op jit(solution)/shard_map/reduce_scatter | solution.py:76
  69.5 65.1 %copy-start.13 = (bf16[256,768]{1,0:T(8,128)(2,1)S(1)}, bf16[256,768]{1,0:T(8,128)(2,1)}, u32[]{:S(2)}) copy-start(bf16[256,768]{1,0:T(8,128)(2,1)} %param.14) | copy-start | bytes 1179652
  71.8 65.7 %copy-start.49 = (bf16[128,768]{1,0:T(8,128)(2,1)S(1)}, bf16[128,768]{1,0:T(8,128)(2,1)}, u32[]{:S(2)}) copy-start(bf16[128,768]{1,0:T(8,128)(2,1)} %param.15) | copy-start | bytes 589828
  71.8 93.9 %copy-start.52 = (bf16[768,2,192]{0,2,1:T(8,128)(2,1)S(1)}, bf16[768,2,192]{0,2,1:T(8,128)(2,1)}, u32[]{:S(2)}) copy-start(bf16[768,2,192]{0,2,1:T(8,128)(2,1)} %param.22) | copy-start | bytes 1769476
  71.8 109.5 %all-gather.9.cloned.1.call-start = ((), (), s32[]{:S(2)}) async-start(), calls=%async_computation.9 | async-start | bytes 1966080 | tf_op jit(solution)/shard_map/all_gather | solution.py:64
  137.4 115.6 %reduce-scatter.10.cloned.1.call-start = ((), (), s32[]{:S(2)}) async-start(), calls=%async_computation.10 | async-start | bytes 3932160 | tf_op jit(solution)/shard_map/reduce_scatter | solution.py:76
  137.4 8.3 collective-permute-start
  145.8 13.5 %collective-permute-start.1 = (bf16[128,768]{1,0:T(8,128)(2,1)S(1)}, bf16[128,768]{1,0:T(8,128)(2,1)S(1)}, u32[]{:S(2)}, u32[]{:S(2)}) collective-permute-start(bf16[128,768]{1,0:T(8,128)(2,1)S(1)} %collective-permute-done), channel_id=1, source_target_pairs={{0,1},{1,2},{2,3},{3,0},{4,5},{5,6},{6,7},{7,4},{8,9},{9,10},{10,1... | collective-permute-start | bytes 589832 | tf_op jit(solution)/shard_map/ppermute | solution.py:250
  145.8 18.6 %collective-permute-start.2 = (bf16[128,768]{1,0:T(8,128)(2,1)S(1)}, bf16[128,768]{1,0:T(8,128)(2,1)S(1)}, u32[]{:S(2)}, u32[]{:S(2)}) collective-permute-start(bf16[128,768]{1,0:T(8,128)(2,1)S(1)} %copy-done.49), channel_id=1, source_target_pairs={{0,3},{1,0},{2,1},{3,2},{4,7},{5,4},{6,5},{7,6},{8,11},{9,8},{10,9... | collective-permute-start | bytes 589832 | tf_op jit(solution)/shard_map/ppermute | solution.py:252
  166.2 340.4 %copy-start.23 = (bf16[512,384]{0,1:T(8,128)(2,1)}, bf16[512,384]{0,1:T(8,128)(2,1)S(1)}, u32[]{:S(2)}) copy-start(bf16[512,384]{0,1:T(8,128)(2,1)S(1)} %convolution_convert_fusion.4) | copy-start | bytes 1179652
  192.4 62.5 %copy-start.87 = (f32[768]{0:T(1024)S(1)}, f32[768]{0:T(1024)}, u32[]{:S(2)}) copy-start(f32[768]{0:T(1024)} %get-tuple-element.18) | copy-start | bytes 9220
  192.4 100.7 %all-gather.11.cloned.1.call-start = ((), (), s32[]{:S(2)}) async-start(), calls=%async_computation.11 | async-start | bytes 1966080 | tf_op jit(solution)/shard_map/all_gather | solution.py:64
  254.9 43.9 %copy-start.99 = (f32[256]{0:T(256)}, f32[256]{0:T(256)S(1)}, u32[]{:S(2)}) copy-start(f32[256]{0:T(256)S(1)} %get-tuple-element.64) | copy-start | bytes 3076
  255.8 74.7 %all-gather.13.cloned.1.call-start = ((), (), s32[]{:S(2)}) async-start(), calls=%async_computation.13 | async-start | bytes 1966080 | tf_op jit(solution)/shard_map/all_gather | solution.py:68
  256.3 144.6 %reduce-scatter.14.cloned.1.call-start = ((), (), s32[]{:S(2)}) async-start(), calls=%async_computation.14 | async-start | bytes 3932160 | tf_op jit(solution)/shard_map/reduce_scatter | solution.py:89
  341.7 121.9 %reduce-scatter.12.cloned.1.call-start = ((), (), s32[]{:S(2)}) async-start(), calls=%async_computation.12 | async-start | bytes 3932160 | tf_op jit(solution)/shard_map/reduce_scatter | solution.py:76
  345.8 117.7 %copy-start.44 = (bf16[256,768]{1,0:T(8,128)(2,1)S(1)}, bf16[256,768]{1,0:T(8,128)(2,1)}, u32[]{:S(2)}) copy-start(bf16[256,768]{1,0:T(8,128)(2,1)} %param.16) | copy-start | bytes 1179652
  345.9 157.9 %all-gather.15.cloned.1.call-start = ((), (), s32[]{:S(2)}) async-start(), calls=%async_computation.15 | async-start | bytes 1966080 | tf_op jit(solution)/shard_map/all_gather | solution.py:68
  466.4 40.2 %copy-start.78 = (f32[3,512]{1,0:T(4,128)S(1)}, f32[3,512]{1,0:T(4,128)}, u32[]{:S(2)}) copy-start(f32[3,512]{1,0:T(4,128)} %copy-done.77) | copy-start | bytes 18436
  466.4 40.2 %copy-start.82 = (f32[3,512]{1,0:T(4,128)S(1)}, f32[3,512]{1,0:T(4,128)}, u32[]{:S(2)}) copy-start(f32[3,512]{1,0:T(4,128)} %copy-done.81) | copy-start | bytes 18436
  466.4 40.2 %copy-start.91 = (pred[512]{0:T(512)(128)(4,1)S(1)}, pred[512]{0:T(512)(128)(4,1)}, u32[]{:S(2)}) copy-start(pred[512]{0:T(512)(128)(4,1)} %copy-done.89) | copy-start | bytes 1540
  466.4 110.1 %reduce-scatter.16.cloned.1.call-start = ((), (), s32[]{:S(2)}) async-start(), calls=%async_computation.16 | async-start | bytes 3932160 | tf_op jit(solution)/shard_map/reduce_scatter | solution.py:89
  517.3 101.1 %copy-start.76 = (bf16[192,768]{1,0:T(8,128)(2,1)S(1)}, bf16[192,768]{1,0:T(8,128)(2,1)}, u32[]{:S(2)}) copy-start(bf16[192,768]{1,0:T(8,128)(2,1)} %param.20) | copy-start | bytes 884740
  517.3 101.1 %all-gather.17.cloned.1.call-start = ((), (), s32[]{:S(2)}) async-start(), calls=%async_computation.17 | async-start | bytes 1966080 | tf_op jit(solution)/shard_map/all_gather | solution.py:68
  581.1 135.4 %reduce-scatter.18.cloned.1.call-start = ((), (), s32[]{:S(2)}) async-start(), calls=%async_computation.18 | async-start | bytes 3932160 | tf_op jit(solution)/shard_map/reduce_scatter | solution.py:89
  643.9 116.0 %reduce-scatter.20.cloned.1.call-start = ((), (), s32[]{:S(2)}) async-start(), calls=%async_computation.19 | async-start | bytes 1966080 | tf_op jit(solution)/shard_map/reduce_scatter | solution.py:302
  651.7 235.9 %all-reduce.3.cloned.1.call-start = ((), (), s32[]{:S(2)}) async-start(), calls=%async_computation.20 | async-start | bytes 18874368 | tf_op jit(solution)/shard_map/psum | solution.py:350
  699.6 58.0 %copy-start.26 = (f32[256,768]{1,0:T(8,128)S(1)}, f32[256,768]{1,0:T(8,128)}, u32[]{:S(2)}) copy-start(f32[256,768]{1,0:T(8,128)} %get-tuple-element.33) | copy-start | bytes 2359300
  699.6 58.0 %copy-start.100 = (f32[256]{0:T(256)S(1)}, f32[256]{0:T(256)}, u32[]{:S(2)}) copy-start(f32[256]{0:T(256)} %get-tuple-element.59) | copy-start | bytes 3076
  (95 other events, 460.8 us)
Sparse Core Ops, SparseCore 0:
  13.0 39.7 all-gather.6
  71.9 62.6 reduce-scatter.7
  137.5 43.7 all-gather.8
  192.5 60.4 reduce-scatter.9
  255.9 37.1 all-gather.10
  294.5 35.9 all-gather.12
  341.8 59.1 reduce-scatter.13
  403.3 60.2 reduce-scatter.11
  466.6 37.1 all-gather.14
  517.4 59.0 reduce-scatter.15
  581.2 37.1 all-gather.16
  644.0 59.1 reduce-scatter.17
  706.6 35.8 reduce-scatter.19
  747.8 139.7 all-reduce.2
